TPU v7x, 32 devices: a whole 2x2x4 slice. The times are simulated.
32 devices in a mesh: freq: 4 (over y, core), tcol: 8 (over z, x).
Axes of the slice: x: 2, y: 2, z: 4, core: 2. Of those that a mesh axis runs over, the one named last changes fastest.
Arguments:
- data: bfloat16 [4, 2, 4096, 128], P('freq', None, 'tcol'), may hold values from -6 to 6
- left_factor: bfloat16 [4, 2, 4096, 256], P('freq', None, 'tcol'), may hold values from -0.25 to 0.25
- right_factor: bfloat16 [4, 2, 4096, 256], P('freq', None, 'tcol'), may hold values from -0.1875 to 0.1875
- ranks: int32 [4, 8, 8], P('freq'), may hold values from 1 to 32
- freq_index: int32 [4], P('freq'), may hold values from 0 to 229
Outputs:
- wavefield: float32 [4, 2, 4096, 128], P('freq', None, 'tcol')
- residual: float32 [4, 2, 4096, 128], P('freq', None, 'tcol')
Inputs may be any that keep to these rules, and one draw needn't show every extreme that they name: `ranks`: the rank of each tile; factor columns at or beyond it are not part of the kernel.
All inputs are finite; a program needn't handle non-finite values.
Results may differ from a plain program's by a relative error of at most 0.006.
Values may be sent and summed in bfloat16 or wider, within the bound.
No kernel may reach another device: no remote copies, remote signals or barrier semaphores. Data moves between devices by JAX's collectives and lax.ppermute only.
A program may use at most 64 MiB of HBM per device.

v0:
```python
import jax
import jax.numpy as jnp
from jax import lax
from jax.sharding import PartitionSpec as P

ITERS = 3


def conj_left(factor, field):
    first = jnp.einsum(
        "ftq,fts->fqs", factor[:, 0], field[:, 0], preferred_element_type=jnp.float32
    )
    second = jnp.einsum(
        "ftq,fts->fqs", factor[:, 1], field[:, 1], preferred_element_type=jnp.float32
    )
    third = jnp.einsum(
        "ftq,fts->fqs", factor[:, 0], field[:, 1], preferred_element_type=jnp.float32
    )
    fourth = jnp.einsum(
        "ftq,fts->fqs", factor[:, 1], field[:, 0], preferred_element_type=jnp.float32
    )
    return jnp.stack([first + second, third - fourth], 1)


def plain_right(factor, coeffs):
    first = jnp.einsum(
        "ftq,fqs->fts", factor[:, 0], coeffs[:, 0], preferred_element_type=jnp.float32
    )
    second = jnp.einsum(
        "ftq,fqs->fts", factor[:, 1], coeffs[:, 1], preferred_element_type=jnp.float32
    )
    third = jnp.einsum(
        "ftq,fqs->fts", factor[:, 0], coeffs[:, 1], preferred_element_type=jnp.float32
    )
    fourth = jnp.einsum(
        "ftq,fqs->fts", factor[:, 1], coeffs[:, 0], preferred_element_type=jnp.float32
    )
    return jnp.stack([first - second, third + fourth], 1)


def body(data, left_factor, right_factor, ranks, freq_index):
    ntile = lax.axis_size("tcol")
    here = lax.axis_index("tcol")
    rank_width = left_factor.shape[3] // ntile
    levels = jnp.arange(rank_width)[None, None, :]
    column_ranks = lax.dynamic_slice_in_dim(ranks, here, 1, 2)[:, :, 0]
    row_ranks = lax.dynamic_slice_in_dim(ranks, here, 1, 1)[:, 0, :]
    colmask = (levels < column_ranks[:, :, None]).astype(jnp.float32).reshape(ranks.shape[0], -1)
    rowmask = (levels < row_ranks[:, :, None]).astype(jnp.float32).reshape(ranks.shape[0], -1)
    damping = (0.1 + 0.9 * freq_index.astype(jnp.float32) / 229.0)[:, None, None, None]
    residual = data.astype(jnp.float32)
    wavefield = jnp.zeros_like(residual)
    direction = jnp.zeros_like(residual)
    image = jnp.zeros_like(residual)
    for step in range(ITERS):
        coeffs = conj_left(left_factor, residual.astype(jnp.bfloat16))
        coeffs = (coeffs * rowmask[:, None, :, None]).astype(jnp.bfloat16)
        arrived = lax.all_to_all(coeffs, "tcol", split_axis=2, concat_axis=2, tiled=True)
        gradient = plain_right(right_factor, arrived) - damping * wavefield
        forward_coeffs = conj_left(right_factor, gradient.astype(jnp.bfloat16))
        forward_coeffs = (forward_coeffs * colmask[:, None, :, None]).astype(jnp.bfloat16)
        forward_arrived = lax.all_to_all(
            forward_coeffs, "tcol", split_axis=2, concat_axis=2, tiled=True
        )
        moved = plain_right(left_factor, forward_arrived)
        partial_sums = jnp.stack(
            [
                jnp.sum(moved * moved + damping * gradient * gradient, axis=(0, 1, 2)),
                jnp.sum(moved * image + damping * gradient * direction, axis=(0, 1, 2)),
                jnp.sum(image * image + damping * direction * direction, axis=(0, 1, 2)),
                jnp.sum(moved * residual - damping * gradient * wavefield, axis=(0, 1, 2)),
                jnp.sum(image * residual - damping * direction * wavefield, axis=(0, 1, 2)),
            ]
        )
        totals = lax.psum(partial_sums, ("freq", "tcol"))
        a11, a12, a22, b1, b2 = (totals[0], totals[1], totals[2], totals[3], totals[4])
        if step == 0:
            alpha = b1 / (1.1 * a11)
            beta = jnp.zeros_like(alpha)
        else:
            first = 1.1 * a11
            second = 1.1 * a22
            determinant = first * second - a12 * a12
            alpha = (b1 * second - a12 * b2) / determinant
            beta = (first * b2 - a12 * b1) / determinant
        direction = alpha * gradient + beta * direction
        image = alpha * moved + beta * image
        wavefield = wavefield + direction
        residual = residual - image
    return (wavefield, residual)


def solution(mesh):
    in_specs = (
        P("freq", None, "tcol", None),
        P("freq", None, "tcol", None),
        P("freq", None, "tcol", None),
        P("freq", None, None),
        P("freq"),
    )
    out_specs = (P("freq", None, "tcol", None), P("freq", None, "tcol", None))
    return jax.shard_map(body, mesh=mesh, in_specs=in_specs, out_specs=out_specs, check_vma=False)
```

profile of v0, /device:TPU:0, one launch (start us, length us, event | category | flops | bytes accessed | tf_op | source)
XLA Modules:
  0.0 213.9 jit_solution(10456277240478988102)
XLA Ops:
  0.7 0.7 copy-done
  1.5 1.2 fusion.116
  2.8 1.2 fusion.118
  5.1 0.8 copy.35
  5.9 7.3 %all-to-all-start = ((bf16[1,2,256,128]{3,1,0,2:T(2,128)(2,1)}), bf16[1,2,256,128]{3,1,0,2:T(2,128)(2,1)S(1)}, u32[]{:S(2)}, u32[]{:S(2)}) async-start(bf16[1,2,256,128]{3,1,0,2:T(2,128)(2,1)} %copy.35), calls=%async_computation | async-start | bytes 262144 | tf_op jit(solution)/shard_map/all_to_all | solution.py:58
  13.8 6.7 %all-to-all-done = bf16[1,2,256,128]{3,1,0,2:T(2,128)(2,1)S(1)} async-done(((bf16[1,2,256,128]{3,1,0,2:T(2,128)(2,1)}), bf16[1,2,256,128]{3,1,0,2:T(2,128)(2,1)S(1)}, u32[]{:S(2)}, u32[]{:S(2)}) %all-to-all-start) | async-done | bytes 131104 | tf_op jit(solution)/shard_map/all_to_all | solution.py:58
  22.5 0.8 copy.38
  23.3 3.4 %all-to-all-start.1 = ((bf16[1,2,256,128]{3,1,0,2:T(2,128)(2,1)}), bf16[1,2,256,128]{3,1,0,2:T(2,128)(2,1)S(1)}, u32[]{:S(2)}, u32[]{:S(2)}) async-start(bf16[1,2,256,128]{3,1,0,2:T(2,128)(2,1)} %copy.38), calls=%async_computation.1 | async-start | bytes 262144 | tf_op jit(solution)/shard_map/all_to_all | solution.py:62
  26.8 7.1 %all-to-all-done.1 = bf16[1,2,256,128]{3,1,0,2:T(2,128)(2,1)S(1)} async-done(((bf16[1,2,256,128]{3,1,0,2:T(2,128)(2,1)}), bf16[1,2,256,128]{3,1,0,2:T(2,128)(2,1)S(1)}, u32[]{:S(2)}, u32[]{:S(2)}) %all-to-all-start.1) | async-done | bytes 131104 | tf_op jit(solution)/shard_map/all_to_all | solution.py:62
  35.1 0.4 fusion.39
  35.5 38.5 %psum.21 = f32[5,128]{1,0:T(8,128)S(1)} all-reduce(f32[5,128]{1,0:T(8,128)S(1)} %stack.179), channel_id=1, replica_groups=mesh['freq'=4,'tcol'=8] {'freq','tcol'}, use_global_device_ids=true, to_apply=%region_4.0 | all-reduce | flops 640 | bytes 5120 | tf_op jit(solution)/shard_map/psum | solution.py:75
  74.7 0.3 fusion.18
  75.0 0.3 fusion.19
  75.5 11.7 %all_to_all.30 = bf16[1,2,256,128]{3,1,0,2:T(2,128)(2,1)S(1)} all-to-all(bf16[1,2,256,128]{3,1,0,2:T(2,128)(2,1)S(1)} %copy.46), channel_id=1, replica_groups=mesh['freq'=4,'tcol'=8] {'tcol'}, dimensions={2} | all-to-all | bytes 262144 | tf_op jit(solution)/shard_map/all_to_all | solution.py:58
  89.5 9.7 %all_to_all.31 = bf16[1,2,256,128]{3,1,0,2:T(2,128)(2,1)S(1)} all-to-all(bf16[1,2,256,128]{3,1,0,2:T(2,128)(2,1)S(1)} %copy.49), channel_id=1, replica_groups=mesh['freq'=4,'tcol'=8] {'tcol'}, dimensions={2} | all-to-all | bytes 262144 | tf_op jit(solution)/shard_map/all_to_all | solution.py:62
  100.4 0.3 add_reduce_fusion.1
  101.0 0.6 subtract_reduce_fusion
  101.7 38.3 %psum.22 = f32[5,128]{1,0:T(8,128)S(1)} all-reduce(f32[5,128]{1,0:T(8,128)S(1)} %stack.197), channel_id=1, replica_groups=mesh['freq'=4,'tcol'=8] {'freq','tcol'}, use_global_device_ids=true, to_apply=%region_10.0 | all-reduce | flops 640 | bytes 5120 | tf_op jit(solution)/shard_map/psum | solution.py:75
  139.9 2.1 fusion.186
  142.0 0.3 fusion.100
  142.3 0.3 fusion.102
  142.5 0.3 fusion.14
  143.3 11.7 %all_to_all.32 = bf16[1,2,256,128]{3,1,0,2:T(2,128)(2,1)S(1)} all-to-all(bf16[1,2,256,128]{3,1,0,2:T(2,128)(2,1)S(1)} %copy.56), channel_id=1, replica_groups=mesh['freq'=4,'tcol'=8] {'tcol'}, dimensions={2} | all-to-all | bytes 262144 | tf_op jit(solution)/shard_map/all_to_all | solution.py:58
  156.2 1.1 fusion.185
  158.2 9.7 %all_to_all.33 = bf16[1,2,256,128]{3,1,0,2:T(2,128)(2,1)S(1)} all-to-all(bf16[1,2,256,128]{3,1,0,2:T(2,128)(2,1)S(1)} %copy.59), channel_id=1, replica_groups=mesh['freq'=4,'tcol'=8] {'tcol'}, dimensions={2} | all-to-all | bytes 262144 | tf_op jit(solution)/shard_map/all_to_all | solution.py:62
  169.1 0.5 copy-done.4
  169.7 0.3 copy-done.3
  169.9 0.7 fusion.37
  170.7 38.3 %psum.23 = f32[5,128]{1,0:T(8,128)S(1)} all-reduce(f32[5,128]{1,0:T(8,128)S(1)} %stack.215), channel_id=1, replica_groups=mesh['freq'=4,'tcol'=8] {'freq','tcol'}, use_global_device_ids=true, to_apply=%region_16.0 | all-reduce | flops 640 | bytes 5120 | tf_op jit(solution)/shard_map/psum | solution.py:75
  209.0 2.0 add_subtract_fusion
  210.9 2.0 copy.63
  213.0 1.0 copy.62
  (91 shorter events, 12.6 us)
Async XLA Ops:
  0.6 0.7 copy-start
  0.6 2.1 copy-start.2
  2.8 1.6 copy-start.8
  5.1 15.6 %copy-start.1 = (bf16[1,2,512,256]{3,2,1,0:T(8,128)(2,1)S(1)}, bf16[1,2,512,256]{3,2,1,0:T(8,128)(2,1)}, u32[]{:S(2)}) copy-start(bf16[1,2,512,256]{3,2,1,0:T(8,128)(2,1)} %param.7) | copy-start | bytes 1572868
  5.9 14.6 %all-to-all-start = ((bf16[1,2,256,128]{3,1,0,2:T(2,128)(2,1)}), bf16[1,2,256,128]{3,1,0,2:T(2,128)(2,1)S(1)}, u32[]{:S(2)}, u32[]{:S(2)}) async-start(bf16[1,2,256,128]{3,1,0,2:T(2,128)(2,1)} %copy.35), calls=%async_computation | async-start | bytes 262144 | tf_op jit(solution)/shard_map/all_to_all | solution.py:58
  23.3 10.7 %all-to-all-start.1 = ((bf16[1,2,256,128]{3,1,0,2:T(2,128)(2,1)}), bf16[1,2,256,128]{3,1,0,2:T(2,128)(2,1)S(1)}, u32[]{:S(2)}, u32[]{:S(2)}) async-start(bf16[1,2,256,128]{3,1,0,2:T(2,128)(2,1)} %copy.38), calls=%async_computation.1 | async-start | bytes 262144 | tf_op jit(solution)/shard_map/all_to_all | solution.py:62
  100.1 0.7 copy-start.5
  100.3 0.7 copy-start.6
  168.6 1.0 copy-start.4
  168.9 1.1 copy-start.3
  169.1 1.5 copy-start.7
where the time goes:
time: 215 us; the launch traced here: 214 us
  blocking collectives  158 us (73%)
  waiting for transfers between devices  13.8 us (6%)
  matrix products  13 us (6%)
  starting transfers between devices  10.7 us (5%)
  local copies, waits for them, and re-layouts  8.86 us (4%)
  other arithmetic  7.88 us (4%)
    psum x3, blocking collectives, body(): totals = lax.psum(partial_sums, ('freq', 'tcol'))  115 us
    all_to_all x2, blocking collectives, body(): lax.all_to_all(coeffs, 'tcol', split_axis=2, concat_axis=2, tiled=True)  23.4 us
    all_to_all x2, blocking collectives, body(): lax.all_to_all(forward_coeffs, 'tcol', split_axis=2, concat_axis=2, tiled...  19.5 us
    all_to_all x1, starting transfers between devices, body(): lax.all_to_all(coeffs, 'tcol', split_axis=2, concat_axis=2, tiled=True)  7.28 us
    all_to_all x1, waiting for transfers between devices, body(): lax.all_to_all(forward_coeffs, 'tcol', split_axis=2, concat_axis=2, tiled...  7.12 us
    all_to_all x1, waiting for transfers between devices, body(): lax.all_to_all(coeffs, 'tcol', split_axis=2, concat_axis=2, tiled=True)  6.69 us
    unnamed x21, local copies, waits for them, and re-layouts  5.08 us
  transfers between devices with their start and end apart: 2, of which 2 were waited for; matrix products, arithmetic and copies ran while one was open for 0% of the time, Pallas kernels for 0%

commit v1 on v0

--- a/solution.py
+++ b/solution.py
@@ -72,7 +72,7 @@
                 jnp.sum(image * residual - damping * direction * wavefield, axis=(0, 1, 2)),
             ]
         )
-        totals = lax.psum(partial_sums, ("freq", "tcol"))
+        totals = lax.psum(lax.psum(partial_sums, "tcol"), "freq")
         a11, a12, a22, b1, b2 = (totals[0], totals[1], totals[2], totals[3], totals[4])
         if step == 0:
             alpha = b1 / (1.1 * a11)

time: 215 us -> 168 us (0.78)
  blocking collectives: 158 us -> 111 us
    psum x3 -> x6, blocking collectives: 115 us -> 71.6 us  [body(): totals = lax.psum(lax.psum(partial_sums, 'tcol'), 'freq')]
    all_to_all x2, blocking collectives: 23.4 us -> 19.5 us  [body(): lax.all_to_all(coeffs, 'tcol', split_axis=2, concat_axis=2, tiled=True)]
where the time goes in v1:
time: 168 us; the launch traced here: 167 us
  blocking collectives  111 us (66%)
  waiting for transfers between devices  13.8 us (8%)
  matrix products  12.9 us (8%)
  starting transfers between devices  10.7 us (6%)
  local copies, waits for them, and re-layouts  8.86 us (5%)
  other arithmetic  7.89 us (5%)
  between operations  1.9 us (1%)
    psum x6, blocking collectives, body(): totals = lax.psum(lax.psum(partial_sums, 'tcol'), 'freq')  71.6 us
    all_to_all x2, blocking collectives, body(): lax.all_to_all(forward_coeffs, 'tcol', split_axis=2, concat_axis=2, tiled...  19.6 us
    all_to_all x2, blocking collectives, body(): lax.all_to_all(coeffs, 'tcol', split_axis=2, concat_axis=2, tiled=True)  19.5 us
    all_to_all x1, starting transfers between devices, body(): lax.all_to_all(coeffs, 'tcol', split_axis=2, concat_axis=2, tiled=True)  7.28 us
    all_to_all x1, waiting for transfers between devices, body(): lax.all_to_all(forward_coeffs, 'tcol', split_axis=2, concat_axis=2, tiled...  7.12 us
    all_to_all x1, waiting for transfers between devices, body(): lax.all_to_all(coeffs, 'tcol', split_axis=2, concat_axis=2, tiled=True)  6.69 us
    unnamed x21, local copies, waits for them, and re-layouts  5.08 us
    all_to_all x1, starting transfers between devices, body(): lax.all_to_all(forward_coeffs, 'tcol', split_axis=2, concat_axis=2, tiled...  3.37 us
  transfers between devices with their start and end apart: 2, of which 2 were waited for; matrix products, arithmetic and copies ran while one was open for 0% of the time, Pallas kernels for 0%

profile of v1, /device:TPU:0, one launch (start us, length us, event | category | flops | bytes accessed | tf_op | source)
XLA Modules:
  0.0 166.8 jit_solution(4391480301424513265)
XLA Ops:
  0.7 0.7 copy-done
  1.5 1.2 fusion.116
  2.8 1.2 fusion.118
  5.1 0.8 copy.35
  5.9 7.3 %all-to-all-start = ((bf16[1,2,256,128]{3,1,0,2:T(2,128)(2,1)}), bf16[1,2,256,128]{3,1,0,2:T(2,128)(2,1)S(1)}, u32[]{:S(2)}, u32[]{:S(2)}) async-start(bf16[1,2,256,128]{3,1,0,2:T(2,128)(2,1)} %copy.35), calls=%async_computation | async-start | bytes 262144 | tf_op jit(solution)/shard_map/all_to_all | solution.py:58
  13.8 6.7 %all-to-all-done = bf16[1,2,256,128]{3,1,0,2:T(2,128)(2,1)S(1)} async-done(((bf16[1,2,256,128]{3,1,0,2:T(2,128)(2,1)}), bf16[1,2,256,128]{3,1,0,2:T(2,128)(2,1)S(1)}, u32[]{:S(2)}, u32[]{:S(2)}) %all-to-all-start) | async-done | bytes 131104 | tf_op jit(solution)/shard_map/all_to_all | solution.py:58
  22.5 0.8 copy.38
  23.3 3.4 %all-to-all-start.1 = ((bf16[1,2,256,128]{3,1,0,2:T(2,128)(2,1)}), bf16[1,2,256,128]{3,1,0,2:T(2,128)(2,1)S(1)}, u32[]{:S(2)}, u32[]{:S(2)}) async-start(bf16[1,2,256,128]{3,1,0,2:T(2,128)(2,1)} %copy.38), calls=%async_computation.1 | async-start | bytes 262144 | tf_op jit(solution)/shard_map/all_to_all | solution.py:62
  26.8 7.1 %all-to-all-done.1 = bf16[1,2,256,128]{3,1,0,2:T(2,128)(2,1)S(1)} async-done(((bf16[1,2,256,128]{3,1,0,2:T(2,128)(2,1)}), bf16[1,2,256,128]{3,1,0,2:T(2,128)(2,1)S(1)}, u32[]{:S(2)}, u32[]{:S(2)}) %all-to-all-start.1) | async-done | bytes 131104 | tf_op jit(solution)/shard_map/all_to_all | solution.py:62
  35.1 0.4 fusion.39
  35.5 18.2 %psum.42 = f32[5,128]{1,0:T(8,128)S(1)} all-reduce(f32[5,128]{1,0:T(8,128)S(1)} %stack.179), channel_id=1, replica_groups=mesh['freq'=4,'tcol'=8] {'tcol'}, use_global_device_ids=true, to_apply=%region_4.0 | all-reduce | flops 640 | bytes 5120 | tf_op jit(solution)/shard_map/psum | solution.py:75
  53.7 5.7 %psum.43 = f32[5,128]{1,0:T(8,128)S(1)} all-reduce(f32[5,128]{1,0:T(8,128)S(1)} %psum.42), channel_id=1, replica_groups=mesh['freq'=4,'tcol'=8] {'freq'}, use_global_device_ids=true, to_apply=%region_5.0 | all-reduce | flops 640 | bytes 5120 | tf_op jit(solution)/shard_map/psum | solution.py:75
  59.5 0.3 fusion.108
  59.8 0.3 fusion.110
  60.9 9.7 %all_to_all.30 = bf16[1,2,256,128]{3,1,0,2:T(2,128)(2,1)S(1)} all-to-all(bf16[1,2,256,128]{3,1,0,2:T(2,128)(2,1)S(1)} %copy.46), channel_id=1, replica_groups=mesh['freq'=4,'tcol'=8] {'tcol'}, dimensions={2} | all-to-all | bytes 262144 | tf_op jit(solution)/shard_map/all_to_all | solution.py:58
  72.9 9.8 %all_to_all.31 = bf16[1,2,256,128]{3,1,0,2:T(2,128)(2,1)S(1)} all-to-all(bf16[1,2,256,128]{3,1,0,2:T(2,128)(2,1)S(1)} %copy.49), channel_id=1, replica_groups=mesh['freq'=4,'tcol'=8] {'tcol'}, dimensions={2} | all-to-all | bytes 262144 | tf_op jit(solution)/shard_map/all_to_all | solution.py:62
  83.8 0.3 add_reduce_fusion.1
  84.5 0.6 subtract_reduce_fusion
  85.1 18.2 %psum.44 = f32[5,128]{1,0:T(8,128)S(1)} all-reduce(f32[5,128]{1,0:T(8,128)S(1)} %stack.197), channel_id=1, replica_groups=mesh['freq'=4,'tcol'=8] {'tcol'}, use_global_device_ids=true, to_apply=%region_11.0 | all-reduce | flops 640 | bytes 5120 | tf_op jit(solution)/shard_map/psum | solution.py:75
  103.3 5.7 %psum.45 = f32[5,128]{1,0:T(8,128)S(1)} all-reduce(f32[5,128]{1,0:T(8,128)S(1)} %psum.44), channel_id=1, replica_groups=mesh['freq'=4,'tcol'=8] {'freq'}, use_global_device_ids=true, to_apply=%region_12.0 | all-reduce | flops 640 | bytes 5120 | tf_op jit(solution)/shard_map/psum | solution.py:75
  109.0 2.1 %fusion.186 = (bf16[1,2,512,128]{2,3,1,0:T(8,128)(2,1)S(1)}, f32[1,2,512,128]{2,3,1,0:T(8,128)S(1)}, f32[1,2,512,128]{2,3,1,0:T(8,128)}) fusion(f32[1,1,512,128]{2,3,1,0:T(8,128)S(1)} %fusion.8, f32[1,1,512,128]{2,3,1,0:T(8,128)S(1)} %fusion.9, f32[128]{0:T(128)S(1)} %fusion.128, bf16[1,2,512,128]{2,3,1,0:T(8,128)(2,1)S(1)} %copy.41, ...), kind=kLoop, calls=%fused_computation.284 | loop fusion | flops 1310720 | bytes 2622976 | tf_op jit(solution)/shard_map/convert_element_type | solution.py:56
  112.4 9.8 %all_to_all.32 = bf16[1,2,256,128]{3,1,0,2:T(2,128)(2,1)S(1)} all-to-all(bf16[1,2,256,128]{3,1,0,2:T(2,128)(2,1)S(1)} %copy.56), channel_id=1, replica_groups=mesh['freq'=4,'tcol'=8] {'tcol'}, dimensions={2} | all-to-all | bytes 262144 | tf_op jit(solution)/shard_map/all_to_all | solution.py:58
  123.3 1.1 fusion.185
  125.4 9.8 %all_to_all.33 = bf16[1,2,256,128]{3,1,0,2:T(2,128)(2,1)S(1)} all-to-all(bf16[1,2,256,128]{3,1,0,2:T(2,128)(2,1)S(1)} %copy.59), channel_id=1, replica_groups=mesh['freq'=4,'tcol'=8] {'tcol'}, dimensions={2} | all-to-all | bytes 262144 | tf_op jit(solution)/shard_map/all_to_all | solution.py:62
  136.4 0.5 copy-done.4
  136.9 0.3 copy-done.3
  137.2 0.7 fusion.37
  137.9 18.2 %psum.46 = f32[5,128]{1,0:T(8,128)S(1)} all-reduce(f32[5,128]{1,0:T(8,128)S(1)} %stack.215), channel_id=1, replica_groups=mesh['freq'=4,'tcol'=8] {'tcol'}, use_global_device_ids=true, to_apply=%region_18.0 | all-reduce | flops 640 | bytes 5120 | tf_op jit(solution)/shard_map/psum | solution.py:75
  156.1 5.7 %psum.47 = f32[5,128]{1,0:T(8,128)S(1)} all-reduce(f32[5,128]{1,0:T(8,128)S(1)} %psum.46), channel_id=1, replica_groups=mesh['freq'=4,'tcol'=8] {'freq'}, use_global_device_ids=true, to_apply=%region_19.0 | all-reduce | flops 640 | bytes 5120 | tf_op jit(solution)/shard_map/psum | solution.py:75
  161.8 2.0 %add_subtract_fusion = (f32[1,2,512,128]{2,3,1,0:T(8,128)}, f32[1,2,512,128]{2,3,1,0:T(8,128)S(1)}) fusion(f32[1,2,512,128]{2,3,1,0:T(8,128)S(1)} %get-tuple-element.25, f32[1,2,512,128]{2,3,1,0:T(8,128)S(1)} %copy-done.3, f32[128]{0:T(128)S(1)} %get-tuple-element.42, f32[128]{0:T(128)S(1)} %get-tuple-element.41, f32[1,1,512,128]{2,3,1,0:T(8,128)} %copy-done.7, ...), kind=kLoop, calls=%fused_computation.85 | loop fusion | flops 1703936 | bytes 4195844 | tf_op jit(solution)/shard_map/sub | solution.py:89
  163.8 2.0 %copy.63 = f32[1,2,512,128]{3,2,1,0:T(8,128)} copy(f32[1,2,512,128]{2,3,1,0:T(8,128)} %get-tuple-element.45) | data formatting | bytes 1048576
  165.8 1.0 copy.62
  (94 shorter events, 13.4 us)
Async XLA Ops:
  0.6 0.7 copy-start
  0.6 2.1 %copy-start.2 = (bf16[1,2,512,256]{3,2,1,0:T(8,128)(2,1)S(1)}, bf16[1,2,512,256]{3,2,1,0:T(8,128)(2,1)}, u32[]{:S(2)}) copy-start(bf16[1,2,512,256]{3,2,1,0:T(8,128)(2,1)} %param.6) | copy-start | bytes 1572868
  2.8 1.6 copy-start.8
  5.1 15.6 %copy-start.1 = (bf16[1,2,512,256]{3,2,1,0:T(8,128)(2,1)S(1)}, bf16[1,2,512,256]{3,2,1,0:T(8,128)(2,1)}, u32[]{:S(2)}) copy-start(bf16[1,2,512,256]{3,2,1,0:T(8,128)(2,1)} %param.7) | copy-start | bytes 1572868
  5.9 14.6 %all-to-all-start = ((bf16[1,2,256,128]{3,1,0,2:T(2,128)(2,1)}), bf16[1,2,256,128]{3,1,0,2:T(2,128)(2,1)S(1)}, u32[]{:S(2)}, u32[]{:S(2)}) async-start(bf16[1,2,256,128]{3,1,0,2:T(2,128)(2,1)} %copy.35), calls=%async_computation | async-start | bytes 262144 | tf_op jit(solution)/shard_map/all_to_all | solution.py:58
  23.3 10.7 %all-to-all-start.1 = ((bf16[1,2,256,128]{3,1,0,2:T(2,128)(2,1)}), bf16[1,2,256,128]{3,1,0,2:T(2,128)(2,1)S(1)}, u32[]{:S(2)}, u32[]{:S(2)}) async-start(bf16[1,2,256,128]{3,1,0,2:T(2,128)(2,1)} %copy.38), calls=%async_computation.1 | async-start | bytes 262144 | tf_op jit(solution)/shard_map/all_to_all | solution.py:62
  83.6 0.7 copy-start.5
  83.8 0.7 copy-start.6
  135.9 1.0 copy-start.4
  136.1 1.1 copy-start.3
  136.4 1.5 copy-start.7
